TPU v7x, 256 devices: a whole 4x4x8 slice. The times are simulated.
256 devices in a mesh: grp: 32 (over z_lo, x, core), shard: 8 (over z_hi, y).
Axes of the slice: x: 4, y: 4, z: 8 (z_hi: 2, z_lo: 4; z = z_hi * 4 + z_lo), core: 2. Of those that a mesh axis runs over, the one named last changes fastest.
Arguments:
- tokens: bfloat16 [16384, 2560], P(('grp', 'shard')), may hold values from -0.125 to 0.125
- target: bfloat16 [16384, 13824], P('grp', 'shard'), may hold values from -6 to 6
- post_mean: float32 [2560, 13824], P('grp', 'shard'), may hold values from -5 to 5
- post_hess: float32 [2560, 13824], P('grp', 'shard'), may hold values from 0.05 to 0.5
- weight_noise: bfloat16 [32, 2560, 13824], P(None, 'grp', 'shard'), may hold values from -6 to 6
Outputs:
- new_mean: float32 [2560, 13824], P('grp', 'shard')
- new_hess: float32 [2560, 13824], P('grp', 'shard')
All inputs are finite; a program needn't handle non-finite values.
Results may differ from a plain program's by a relative error of at most 0.0018.
Values may be sent and summed in bfloat16 or wider, within the bound.
A program may use at most 192 MiB of HBM per device.

v0:
```python
import jax
import jax.numpy as jnp
from jax import lax
from jax.sharding import PartitionSpec as P

sample_size = 50.0
weight_decay = 0.02
hess_decay = 0.95
learn_rate = 0.3


def contract_rows(left, right):
    return lax.dot_general(
        left, right, (((0,), (0,)), ((), ())), preferred_element_type=jnp.float32
    )


def local(tokens, target, post_mean, post_hess, weight_noise):
    groups = weight_noise.shape[0]
    post_std = lax.rsqrt(sample_size * (post_hess + weight_decay))
    noise_vals = weight_noise.astype(jnp.float32)
    samples = (post_mean[None] + post_std[None] * noise_vals).astype(jnp.bfloat16)
    group_x = lax.all_gather(tokens, "shard", axis=0, tiled=True)
    output = jnp.dot(
        group_x,
        lax.all_to_all(samples, "grp", split_axis=0, concat_axis=1, tiled=True)[0],
        preferred_element_type=jnp.float32,
    )
    residual = (output - target.astype(jnp.float32)).astype(jnp.bfloat16)
    gradient = contract_rows(group_x, residual).astype(jnp.bfloat16)
    group_grads = lax.all_to_all(gradient[None], "grp", split_axis=1, concat_axis=0, tiled=True)
    group_grads = group_grads.astype(jnp.float32)
    mean_grad = jnp.sum(group_grads, axis=0) / groups
    hess_est = jnp.sum(group_grads * noise_vals, axis=0) / groups / post_std
    keep_rate = 1.0 - hess_decay
    gap = post_hess - hess_est
    new_hess = (
        hess_decay * post_hess
        + keep_rate * hess_est
        + 0.5 * keep_rate * keep_rate * gap * gap / (post_hess + weight_decay)
    )
    new_mean = post_mean - learn_rate * (mean_grad + weight_decay * post_mean) / (
        new_hess + weight_decay
    )
    return (new_mean, new_hess)


def solution(mesh):
    return jax.shard_map(
        local,
        mesh=mesh,
        in_specs=(
            P(("grp", "shard"), None),
            P("grp", "shard"),
            P("grp", "shard"),
            P("grp", "shard"),
            P(None, "grp", "shard"),
        ),
        out_specs=(P("grp", "shard"), P("grp", "shard")),
        check_vma=False,
    )
```

profile of v0, /device:TPU:1, one launch (start us, length us, event | category | flops | bytes accessed | tf_op | source)
XLA Modules:
  0.0 707.4 jit_solution(3777936069902256427)
XLA Ops:
  7.2 1.1 multiply_rsqrt_fusion
  8.3 9.5 %fusion.1 = bf16[32,80,1728]{2,1,0:T(8,128)(2,1)} fusion(bf16[32,80,1728]{2,1,0:T(8,128)(2,1)} %param.9, f32[80,1728]{1,0:T(8,128)S(1)} %multiply_rsqrt_fusion, f32[80,1728]{1,0:T(8,128)} %param.7), kind=kLoop, calls=%fused_computation.4 | loop fusion | flops 17694720 | bytes 18800640 | tf_op jit(solution)/shard_map/convert_element_type | solution.py:22
  17.8 0.0 copy-start.2
  17.8 10.2 %all-to-all-start = ((bf16[32,80,1728]{2,1,0:T(8,128)(2,1)}), bf16[32,80,1728]{2,1,0:T(8,128)(2,1)}, u32[]{:S(2)}, u32[]{:S(2)}) async-start(bf16[32,80,1728]{2,1,0:T(8,128)(2,1)} %fusion.1), calls=%async_computation | async-start | bytes 18350080 | tf_op jit(solution)/shard_map/all_to_all | solution.py:26
  28.0 0.2 all-gather.2.cloned.1.call-start
  28.2 0.5 all-gather.2.cloned.1.call-update
  28.7 108.1 %all-gather.2.cloned.1.call-done = bf16[512,2560]{1,0:T(8,128)(2,1)} async-done(((bf16[64,2560]{1,0:T(8,128)(2,1)}), bf16[512,2560]{1,0:T(8,128)(2,1)}) %all-gather.2.cloned.1.call-update) | async-done | bytes 2621456 | tf_op jit(solution)/shard_map/all_gather | solution.py:23
  136.9 129.7 %all-to-all-done = bf16[32,80,1728]{2,1,0:T(8,128)(2,1)} async-done(((bf16[32,80,1728]{2,1,0:T(8,128)(2,1)}), bf16[32,80,1728]{2,1,0:T(8,128)(2,1)}, u32[]{:S(2)}, u32[]{:S(2)}) %all-to-all-start) | async-done | bytes 8847392 | tf_op jit(solution)/shard_map/all_to_all | solution.py:26
  266.5 0.0 copy-done.2
  266.5 17.0 %fusion.3 = bf16[1,2560,1728]{1,2,0:T(8,128)(2,1)} fusion(bf16[512,2560]{1,0:T(8,128)(2,1)} %all-gather.2.cloned.1.call-done, bf16[512,1728]{0,1:T(8,128)(2,1)S(1)} %copy-done.2, bf16[2560,1728]{1,0:T(8,128)(2,1)} %bitcast), kind=kOutput, calls=%fused_computation.7 | convolution fusion | flops 9066774528 | bytes 22085632 | tf_op jit(solution)/shard_map/dot_general | solution.py:13
  283.6 37.2 %copy.9 = bf16[1,2560,1728]{2,0,1:T(2,128)(2,1)} copy(bf16[1,2560,1728]{1,2,0:T(8,128)(2,1)} %fusion.3) | data formatting | bytes 17694720 | tf_op jit(solution)/shard_map/broadcast_in_dim | solution.py:31
  320.7 0.5 broadcast.21
  321.2 101.7 %reduce = bf16[2560,1728]{1,0:T(8,128)(2,1)} reduce(bf16[2560,1,1728]{2,1,0:T(2,128)(2,1)} %bitcast.18, bf16[]{:T(256)} %broadcast.21), dimensions={1}, to_apply=%bitcast.13.reduce_sub_computation | reduce | bytes 17694722
  422.9 24.1 %reshape.16 = bf16[32,2,69120]{2,1,0:T(2,128)(2,1)} reshape(bf16[2560,1728]{1,0:T(8,128)(2,1)} %reduce) | data formatting | bytes 17694720
  447.0 200.5 %all_to_all.8 = bf16[32,2,69120]{2,1,0:T(2,128)(2,1)} all-to-all(bf16[32,2,69120]{2,1,0:T(2,128)(2,1)} %reshape.16), channel_id=1, replica_groups=mesh['grp'=32,'shard'=8] {'grp'}, dimensions={0} | all-to-all | bytes 17694720 | tf_op jit(solution)/shard_map/all_to_all | solution.py:31
  647.5 27.7 %reshape.17 = bf16[2560,1,1728]{2,1,0:T(2,128)(2,1)} reshape(bf16[32,2,69120]{2,1,0:T(2,128)(2,1)} %all_to_all.8) | data formatting | bytes 17694720
  675.3 14.1 %copy.10 = bf16[1,2560,1728]{2,1,0:T(8,128)(2,1)} copy(bf16[1,2560,1728]{2,0,1:T(2,128)(2,1)} %bitcast.19) | data formatting | bytes 17694720 | tf_op jit(solution)/shard_map/all_to_all | solution.py:31
  689.4 0.0 copy-start
  689.4 0.0 copy-start.1
  689.4 9.7 %convert_reduce_fusion = (f32[80,1728]{1,0:T(8,128)S(1)}, f32[80,1728]{1,0:T(8,128)S(1)}) fusion(bf16[32,80,1728]{2,1,0:T(8,128)(2,1)} %bitcast.20, bf16[32,80,1728]{2,1,0:T(8,128)(2,1)} %param.9), kind=kLoop, calls=%fused_computation.1 | loop fusion | flops 21841920 | bytes 18800640 | tf_op jit(solution)/shard_map/reduce_sum | solution.py:33
  699.1 0.0 copy-done
  699.1 0.0 copy-done.1
  699.1 1.4 divide_subtract_fusion
Async XLA Ops:
  17.8 248.8 %copy-start.2 = (bf16[512,1728]{0,1:T(8,128)(2,1)S(1)}, bf16[512,1728]{0,1:T(8,128)(2,1)}, u32[]{:S(2)}) copy-start(bf16[512,1728]{0,1:T(8,128)(2,1)} %param.6) | copy-start | bytes 5308420
  17.8 248.8 %all-to-all-start = ((bf16[32,80,1728]{2,1,0:T(8,128)(2,1)}), bf16[32,80,1728]{2,1,0:T(8,128)(2,1)}, u32[]{:S(2)}, u32[]{:S(2)}) async-start(bf16[32,80,1728]{2,1,0:T(8,128)(2,1)} %fusion.1), calls=%async_computation | async-start | bytes 18350080 | tf_op jit(solution)/shard_map/all_to_all | solution.py:26
  28.0 108.9 %all-gather.2.cloned.1.call-start = ((), (), s32[]{:S(2)}) async-start(), calls=%async_computation.2 | async-start | bytes 2949120 | tf_op jit(solution)/shard_map/all_gather | solution.py:23
  689.4 9.7 %copy-start = (f32[80,1728]{1,0:T(8,128)S(1)}, f32[80,1728]{1,0:T(8,128)}, u32[]{:S(2)}) copy-start(f32[80,1728]{1,0:T(8,128)} %param.7) | copy-start | bytes 1658884
  689.4 9.8 %copy-start.1 = (f32[80,1728]{1,0:T(8,128)S(1)}, f32[80,1728]{1,0:T(8,128)}, u32[]{:S(2)}) copy-start(f32[80,1728]{1,0:T(8,128)} %param.8) | copy-start | bytes 1658884
Sparse Core Ops, SparseCore 0:
  31.4 105.4 all-gather.1
where the time goes:
time: 710 us; the launch traced here: 707 us
  waiting for transfers between devices  238 us (34%)
  blocking collectives  201 us (28%)
  other arithmetic  123 us (17%)
  local copies, waits for them, and re-layouts  104 us (15%)
  matrix products  17 us (2%)
  between operations  14.1 us (2%)
  starting transfers between devices  10.4 us (1%)
    all_to_all x1, blocking collectives, local(): lax.all_to_all(gradient[None], 'grp', split_axis=1, concat_axis=0, tiled=...  201 us
    all_to_all x1, waiting for transfers between devices, local(): lax.all_to_all(samples, 'grp', split_axis=0, concat_axis=1, tiled=True)[0]  130 us
    all_gather x1, waiting for transfers between devices, local(): group_x = lax.all_gather(tokens, 'shard', axis=0, tiled=True)  108 us
    unnamed x1, other arithmetic  102 us
    unnamed x9, local copies, waits for them, and re-layouts  52.4 us
    broadcast_in_dim x1, local copies, waits for them, and re-layouts, local(): gradient[None]  37.2 us
    dot_general x1, matrix products, contract_rows(): lax.dot_general(left, right, (((0,), (0,)), ((), ())), preferred_element_...  17 us
  transfers between devices with their start and end apart: 2, of which 2 were waited for; matrix products, arithmetic and copies ran while one was open for 0% of the time, Pallas kernels for 0%

commit v1 on v0

--- a/solution.py
+++ b/solution.py
@@ -20,7 +20,10 @@
     post_std = lax.rsqrt(sample_size * (post_hess + weight_decay))
     noise_vals = weight_noise.astype(jnp.float32)
     samples = (post_mean[None] + post_std[None] * noise_vals).astype(jnp.bfloat16)
-    group_x = lax.all_gather(tokens, "shard", axis=0, tiled=True)
+    n_dev = lax.axis_size("shard")
+    pieces = jnp.stack([tokens for _ in range(n_dev)])
+    pieces = lax.all_to_all(pieces, "shard", split_axis=0, concat_axis=0)
+    group_x = jnp.concatenate(pieces, axis=0)
     output = jnp.dot(
         group_x,
         lax.all_to_all(samples, "grp", split_axis=0, concat_axis=1, tiled=True)[0],

time: 710 us -> 718 us (1.011)
  blocking collectives: 201 us -> 428 us
  waiting for transfers between devices: 238 us -> 30.3 us
  between operations: 14.1 us -> 0.66 us
    all_to_all x0 -> x1, blocking collectives: none -> 228 us  [local(): lax.all_to_all(samples, 'grp', split_axis=0, concat_axis=1, tiled=True)[0]]
    all_gather x1 -> x0, waiting for transfers between devices: 108 us -> none  [local(): group_x = lax.all_gather(tokens, 'shard', axis=0, tiled=True)]
    all_to_all x1, waiting for transfers between devices: 130 us -> 30.3 us  [local(): pieces = lax.all_to_all(pieces, 'shard', split_axis=0, concat_axis=0)]
    unnamed x9 -> x7, local copies, waits for them, and re-layouts: 52.4 us -> 52.4 us
  transfers between devices with their start and end apart: 2 -> 1, of which waited for: 2 -> 1; matrix products, arithmetic and copies ran while one was open for 0% -> 2% of each run, Pallas kernels for 0% -> 0%
where the time goes in v1:
time: 718 us; the launch traced here: 716 us
  blocking collectives  428 us (60%)
  other arithmetic  124 us (17%)
  local copies, waits for them, and re-layouts  106 us (15%)
  waiting for transfers between devices  30.3 us (4%)
  matrix products  14.5 us (2%)
  starting transfers between devices  11.6 us (2%)
    all_to_all x1, blocking collectives, local(): lax.all_to_all(samples, 'grp', split_axis=0, concat_axis=1, tiled=True)[0]  228 us
    all_to_all x1, blocking collectives, local(): lax.all_to_all(gradient[None], 'grp', split_axis=1, concat_axis=0, tiled=...  200 us
    unnamed x1, other arithmetic  102 us
    unnamed x7, local copies, waits for them, and re-layouts  52.4 us
    broadcast_in_dim x1, local copies, waits for them, and re-layouts, local(): gradient[None]  37.2 us
    all_to_all x1, waiting for transfers between devices, local(): pieces = lax.all_to_all(pieces, 'shard', split_axis=0, concat_axis=0)  30.3 us
    dot_general x1, matrix products, contract_rows(): lax.dot_general(left, right, (((0,), (0,)), ((), ())), preferred_element_...  14.5 us
  transfers between devices with their start and end apart: 1, of which 1 were waited for; matrix products, arithmetic and copies ran while one was open for 2% of the time, Pallas kernels for 0%

profile of v1, /device:TPU:1, one launch (start us, length us, event | category | flops | bytes accessed | tf_op | source)
XLA Modules:
  0.0 715.8 jit_solution(14909158271878799778)
XLA Ops:
  0.6 0.0 copy-start
  0.6 2.7 stack.2
  3.4 11.6 %all-to-all-start.1 = ((bf16[8,64,2560]{2,1,0:T(8,128)(2,1)}), bf16[8,64,2560]{2,1,0:T(8,128)(2,1)S(1)}, u32[]{:S(2)}, u32[]{:S(2)}) async-start(bf16[8,64,2560]{2,1,0:T(8,128)(2,1)} %stack.2), calls=%async_computation.1 | async-start | bytes 5242880 | tf_op jit(solution)/shard_map/all_to_all | solution.py:25
  15.0 1.9 multiply_rsqrt_fusion
  16.9 0.0 copy-done
  17.0 9.4 %fusion.1 = bf16[32,80,1728]{2,1,0:T(8,128)(2,1)} fusion(bf16[32,80,1728]{2,1,0:T(8,128)(2,1)} %param.9, f32[80,1728]{1,0:T(8,128)} %multiply_rsqrt_fusion, f32[80,1728]{1,0:T(8,128)S(1)} %copy-done), kind=kLoop, calls=%fused_computation.4 | loop fusion | flops 17694720 | bytes 18800640 | tf_op jit(solution)/shard_map/convert_element_type | solution.py:22
  26.4 30.3 %all-to-all-done.1 = bf16[8,64,2560]{2,1,0:T(8,128)(2,1)S(1)} async-done(((bf16[8,64,2560]{2,1,0:T(8,128)(2,1)}), bf16[8,64,2560]{2,1,0:T(8,128)(2,1)S(1)}, u32[]{:S(2)}, u32[]{:S(2)}) %all-to-all-start.1) | async-done | bytes 2621472 | tf_op jit(solution)/shard_map/all_to_all | solution.py:25
  56.7 228.4 %all_to_all.23 = bf16[32,80,1728]{2,1,0:T(8,128)(2,1)} all-to-all(bf16[32,80,1728]{2,1,0:T(8,128)(2,1)} %fusion.1), channel_id=1, replica_groups=mesh['grp'=32,'shard'=8] {'grp'}, dimensions={0} | all-to-all | bytes 17694720 | tf_op jit(solution)/shard_map/all_to_all | solution.py:29
  285.1 14.5 %fusion.3 = bf16[1,2560,1728]{1,2,0:T(8,128)(2,1)} fusion(bf16[512,2560]{1,0:T(8,128)(2,1)S(1)} %bitcast.23, bf16[512,1728]{0,1:T(8,128)(2,1)} %param.6, bf16[2560,1728]{1,0:T(8,128)(2,1)} %bitcast.22), kind=kOutput, calls=%fused_computation.7 | convolution fusion | flops 9066774528 | bytes 22085632 | tf_op jit(solution)/shard_map/dot_general | solution.py:13
  299.7 37.2 %copy.9 = bf16[1,2560,1728]{2,0,1:T(2,128)(2,1)} copy(bf16[1,2560,1728]{1,2,0:T(8,128)(2,1)} %fusion.3) | data formatting | bytes 17694720 | tf_op jit(solution)/shard_map/broadcast_in_dim | solution.py:34
  336.9 0.5 broadcast.23
  337.5 101.7 %reduce = bf16[2560,1728]{1,0:T(8,128)(2,1)} reduce(bf16[2560,1,1728]{2,1,0:T(2,128)(2,1)} %bitcast.19, bf16[]{:T(256)} %broadcast.23), dimensions={1}, to_apply=%bitcast.14.reduce_sub_computation | reduce | bytes 17694722
  439.1 24.1 %reshape.22 = bf16[32,2,69120]{2,1,0:T(2,128)(2,1)} reshape(bf16[2560,1728]{1,0:T(8,128)(2,1)} %reduce) | data formatting | bytes 17694720
  463.2 199.5 %all_to_all.24 = bf16[32,2,69120]{2,1,0:T(2,128)(2,1)} all-to-all(bf16[32,2,69120]{2,1,0:T(2,128)(2,1)} %reshape.22), channel_id=1, replica_groups=mesh['grp'=32,'shard'=8] {'grp'}, dimensions={0} | all-to-all | bytes 17694720 | tf_op jit(solution)/shard_map/all_to_all | solution.py:34
  662.8 27.8 %reshape.23 = bf16[2560,1,1728]{2,1,0:T(2,128)(2,1)} reshape(bf16[32,2,69120]{2,1,0:T(2,128)(2,1)} %all_to_all.24) | data formatting | bytes 17694720
  690.6 14.1 %copy.10 = bf16[1,2560,1728]{2,1,0:T(8,128)(2,1)} copy(bf16[1,2560,1728]{2,0,1:T(2,128)(2,1)} %bitcast.20) | data formatting | bytes 17694720 | tf_op jit(solution)/shard_map/all_to_all | solution.py:34
  704.6 0.0 copy-start.1
  704.6 9.7 %convert_reduce_fusion = (f32[80,1728]{1,0:T(8,128)S(1)}, f32[80,1728]{1,0:T(8,128)S(1)}) fusion(bf16[32,80,1728]{2,1,0:T(8,128)(2,1)} %bitcast.21, bf16[32,80,1728]{2,1,0:T(8,128)(2,1)} %param.9), kind=kLoop, calls=%fused_computation.1 | loop fusion | flops 21841920 | bytes 18800640 | tf_op jit(solution)/shard_map/reduce_sum | solution.py:36
  714.3 0.0 copy-done.1
  714.4 1.4 divide_subtract_fusion
Async XLA Ops:
  0.6 16.3 %copy-start = (f32[80,1728]{1,0:T(8,128)S(1)}, f32[80,1728]{1,0:T(8,128)}, u32[]{:S(2)}) copy-start(f32[80,1728]{1,0:T(8,128)} %param.7) | copy-start | bytes 1658884
  3.4 53.4 %all-to-all-start.1 = ((bf16[8,64,2560]{2,1,0:T(8,128)(2,1)}), bf16[8,64,2560]{2,1,0:T(8,128)(2,1)S(1)}, u32[]{:S(2)}, u32[]{:S(2)}) async-start(bf16[8,64,2560]{2,1,0:T(8,128)(2,1)} %stack.2), calls=%async_computation.1 | async-start | bytes 5242880 | tf_op jit(solution)/shard_map/all_to_all | solution.py:25
  704.6 9.7 %copy-start.1 = (f32[80,1728]{1,0:T(8,128)S(1)}, f32[80,1728]{1,0:T(8,128)}, u32[]{:S(2)}) copy-start(f32[80,1728]{1,0:T(8,128)} %param.8) | copy-start | bytes 1658884

commit v2 on v0

--- a/solution.py
+++ b/solution.py
@@ -28,7 +28,11 @@
     )
     residual = (output - target.astype(jnp.float32)).astype(jnp.bfloat16)
     gradient = contract_rows(group_x, residual).astype(jnp.bfloat16)
-    group_grads = lax.all_to_all(gradient[None], "grp", split_axis=1, concat_axis=0, tiled=True)
+    part = gradient[None]
+    size = lax.axis_size("grp")
+    shards = jnp.stack(jnp.split(part, size, axis=1), axis=0)
+    shards = lax.all_to_all(shards, "grp", split_axis=0, concat_axis=0)
+    group_grads = jnp.concatenate(shards, axis=0)
     group_grads = group_grads.astype(jnp.float32)
     mean_grad = jnp.sum(group_grads, axis=0) / groups
     hess_est = jnp.sum(group_grads * noise_vals, axis=0) / groups / post_std

time: 710 us -> 578 us (0.81)
  other arithmetic: 123 us -> 26.1 us
  local copies, waits for them, and re-layouts: 104 us -> 63.8 us
    unnamed x1 -> x0, other arithmetic: 102 us -> none
    broadcast_in_dim x1 -> x0, local copies, waits for them, and re-layouts: 37.2 us -> none  [local(): gradient[None]]
    another operation x0 -> x2, local copies, waits for them, and re-layouts: none -> 16.2 us  [local(): shards = jnp.stack(jnp.split(part, size, axis=1), axis=0)]
    all_to_all x1 -> x0, local copies, waits for them, and re-layouts: 14.1 us -> none  [local(): lax.all_to_all(gradient[None], 'grp', split_axis=1, concat_axis=0, tiled=...]
    reduce_sum x0 -> x1, other arithmetic: none -> 8.77 us  [local(): hess_est = jnp.sum(group_grads * noise_vals, axis=0) / groups / post_std]
    unnamed x9 -> x39, local copies, waits for them, and re-layouts: 52.4 us -> 47.6 us
where the time goes in v2:
time: 578 us; the launch traced here: 577 us
  waiting for transfers between devices  238 us (41%)
  blocking collectives  207 us (36%)
  local copies, waits for them, and re-layouts  63.8 us (11%)
  other arithmetic  26.1 us (5%)
  matrix products  17.2 us (3%)
  between operations  14.1 us (2%)
  starting transfers between devices  10.4 us (2%)
    all_to_all x1, blocking collectives, local(): shards = lax.all_to_all(shards, 'grp', split_axis=0, concat_axis=0)  207 us
    all_to_all x1, waiting for transfers between devices, local(): lax.all_to_all(samples, 'grp', split_axis=0, concat_axis=1, tiled=True)[0]  130 us
    all_gather x1, waiting for transfers between devices, local(): group_x = lax.all_gather(tokens, 'shard', axis=0, tiled=True)  108 us
    unnamed x39, local copies, waits for them, and re-layouts  47.6 us
    dot_general x1, matrix products, contract_rows(): lax.dot_general(left, right, (((0,), (0,)), ((), ())), preferred_element_...  17.2 us
    another operation x2, local copies, waits for them, and re-layouts, local(): shards = jnp.stack(jnp.split(part, size, axis=1), axis=0)  16.2 us
  transfers between devices with their start and end apart: 2, of which 2 were waited for; matrix products, arithmetic and copies ran while one was open for 0% of the time, Pallas kernels for 0%

profile of v2, /device:TPU:1, one launch (start us, length us, event | category | flops | bytes accessed | tf_op | source)
XLA Modules:
  0.0 576.9 jit_solution(7195888307463575802)
XLA Ops:
  7.2 1.1 multiply_rsqrt_fusion
  8.3 9.4 %fusion.1 = bf16[32,80,1728]{2,1,0:T(8,128)(2,1)} fusion(bf16[32,80,1728]{2,1,0:T(8,128)(2,1)} %param.9, f32[80,1728]{1,0:T(8,128)S(1)} %multiply_rsqrt_fusion, f32[80,1728]{1,0:T(8,128)} %param.7), kind=kLoop, calls=%fused_computation.5 | loop fusion | flops 17694720 | bytes 18800640 | tf_op jit(solution)/shard_map/convert_element_type | solution.py:22
  17.7 10.2 %all-to-all-start = ((bf16[32,80,1728]{2,1,0:T(8,128)(2,1)}), bf16[32,80,1728]{2,1,0:T(8,128)(2,1)}, u32[]{:S(2)}, u32[]{:S(2)}) async-start(bf16[32,80,1728]{2,1,0:T(8,128)(2,1)} %fusion.1), calls=%async_computation | async-start | bytes 18350080 | tf_op jit(solution)/shard_map/all_to_all | solution.py:26
  28.6 108.1 %all-gather.2.cloned.1.call-done = bf16[512,2560]{1,0:T(8,128)(2,1)} async-done(((bf16[64,2560]{1,0:T(8,128)(2,1)}), bf16[512,2560]{1,0:T(8,128)(2,1)}) %all-gather.2.cloned.1.call-update) | async-done | bytes 2621456 | tf_op jit(solution)/shard_map/all_gather | solution.py:23
  136.8 129.7 %all-to-all-done = bf16[32,80,1728]{2,1,0:T(8,128)(2,1)} async-done(((bf16[32,80,1728]{2,1,0:T(8,128)(2,1)}), bf16[32,80,1728]{2,1,0:T(8,128)(2,1)}, u32[]{:S(2)}, u32[]{:S(2)}) %all-to-all-start) | async-done | bytes 8847392 | tf_op jit(solution)/shard_map/all_to_all | solution.py:26
  266.4 17.2 %fusion.3 = bf16[1,2560,1728]{1,2,0:T(8,128)(2,1)} fusion(bf16[512,2560]{1,0:T(8,128)(2,1)} %all-gather.2.cloned.1.call-done, bf16[512,1728]{0,1:T(8,128)(2,1)S(1)} %copy-done.3, bf16[2560,1728]{1,0:T(8,128)(2,1)} %bitcast), kind=kOutput, calls=%fused_computation.8 | convolution fusion | flops 9066774528 | bytes 22085632 | tf_op jit(solution)/shard_map/dot_general | solution.py:13
  283.6 2.0 fusion.38
  285.6 2.8 fusion.37
  288.4 2.0 fusion.36
  290.4 2.1 fusion.35
  292.5 2.1 fusion.34
  294.6 2.0 fusion.33
  296.6 2.1 fusion.32
  298.8 2.0 fusion.31
  300.7 1.8 fusion.30
  302.5 2.1 fusion.29
  304.6 2.0 fusion.28
  306.6 2.1 fusion.27
  308.7 2.2 fusion.26
  310.9 2.0 fusion.25
  312.9 2.1 fusion.24
  315.0 2.0 fusion.23
  318.7 1.0 fusion.20
  319.7 1.0 fusion.19
  320.7 1.0 fusion.18
  322.7 1.0 fusion.16
  329.3 1.0 fusion.9
  332.2 15.3 %copy.26 = bf16[32,1,80,1728]{3,2,1,0:T(8,128)(2,1)} copy(bf16[32,1,80,1728]{2,3,1,0:T(8,128)(2,1)} %fusion.7) | data formatting | bytes 17694720 | tf_op jit(solution)/shard_map/stack | solution.py:33
  347.5 207.0 %all_to_all.14 = bf16[32,1,80,1728]{3,2,1,0:T(8,128)(2,1)} all-to-all(bf16[32,1,80,1728]{3,2,1,0:T(8,128)(2,1)} %copy.26), channel_id=1, replica_groups=mesh['grp'=32,'shard'=8] {'grp'}, dimensions={0} | all-to-all | bytes 17694720 | tf_op jit(solution)/shard_map/all_to_all | solution.py:34
  554.5 8.8 %fusion.2 = f32[80,1728]{1,0:T(8,128)S(1)} fusion(bf16[32,80,1728]{2,1,0:T(8,128)(2,1)} %param.9, bf16[32,1,80,1728]{3,2,1,0:T(8,128)(2,1)} %all_to_all.14), kind=kLoop, calls=%fused_computation.6 | loop fusion | flops 17556480 | bytes 18247680 | tf_op jit(solution)/shard_map/reduce_sum | solution.py:38
  563.3 5.3 convert_reduce_fusion
  568.6 1.4 divide_subtract_fusion
  (21 shorter events, 11.0 us)
Async XLA Ops:
  17.7 248.8 %copy-start.3 = (bf16[512,1728]{0,1:T(8,128)(2,1)S(1)}, bf16[512,1728]{0,1:T(8,128)(2,1)}, u32[]{:S(2)}) copy-start(bf16[512,1728]{0,1:T(8,128)(2,1)} %param.6) | copy-start | bytes 5308420
  17.7 248.8 %all-to-all-start = ((bf16[32,80,1728]{2,1,0:T(8,128)(2,1)}), bf16[32,80,1728]{2,1,0:T(8,128)(2,1)}, u32[]{:S(2)}, u32[]{:S(2)}) async-start(bf16[32,80,1728]{2,1,0:T(8,128)(2,1)} %fusion.1), calls=%async_computation | async-start | bytes 18350080 | tf_op jit(solution)/shard_map/all_to_all | solution.py:26
  27.9 108.9 %all-gather.2.cloned.1.call-start = ((), (), s32[]{:S(2)}) async-start(), calls=%async_computation.2 | async-start | bytes 2949120 | tf_op jit(solution)/shard_map/all_gather | solution.py:23
  283.6 33.3 %copy-start = (bf16[1,2560,1728]{1,2,0:T(8,128)(2,1)S(1)}, bf16[1,2560,1728]{1,2,0:T(8,128)(2,1)}, u32[]{:S(2)}) copy-start(bf16[1,2560,1728]{1,2,0:T(8,128)(2,1)} %fusion.3) | copy-start | bytes 26542084
  554.5 14.1 %copy-start.1 = (f32[80,1728]{1,0:T(8,128)S(1)}, f32[80,1728]{1,0:T(8,128)}, u32[]{:S(2)}) copy-start(f32[80,1728]{1,0:T(8,128)} %param.7) | copy-start | bytes 1658884
  554.5 14.1 %copy-start.2 = (f32[80,1728]{1,0:T(8,128)S(1)}, f32[80,1728]{1,0:T(8,128)}, u32[]{:S(2)}) copy-start(f32[80,1728]{1,0:T(8,128)} %param.8) | copy-start | bytes 1658884
Sparse Core Ops, SparseCore 0:
  31.3 105.4 all-gather.1
